TPU v7x, 32 devices: a whole 2x2x4 slice. The times are simulated.
32 devices in a mesh: row: 8 (over y, x, core), section: 4 (over z).
Axes of the slice: x: 2, y: 2, z: 4, core: 2. Of those that a mesh axis runs over, the one named last changes fastest.
Arguments:
- features: bfloat16 [8192, 256], P('row'), may hold values from -6 to 6
- weight: bfloat16 [256, 256], replicated, may hold values from -0.375 to 0.375
- cotangent: bfloat16 [8192, 256], P('row'), may hold values from -0.0625 to 0.0625
- counts: int32 [64, 16, 128, 128], P('row', 'section'), may hold values from 0 to 3, as said below
- columns: int32 [64, 16], P('row', 'section'), may hold values from 0 to 63, as said below
- live_slots: int32 [64, 4], P('row', 'section'), may hold values from 1 to 4, as said below
Outputs:
- output: bfloat16 [8192, 256], P('row')
- grad_weight: float32 [256, 256], replicated
Inputs may be any that keep to these rules, and one draw needn't show every extreme that they name: `columns`: every entry in a slot of section index s names a node block g with (g // 8) % 4 == s; the 4 slots of one row of blocks and one section index name distinct column blocks. Slots at k >= live_slots[b, s] are ignored; the value 4 occurs at every section index in every draw. `counts`: most entries are zero.
All inputs are finite; a program needn't handle non-finite values.
Results may differ from a plain program's by a relative error of at most 0.0055.
Values may be sent and summed in bfloat16 or wider, within the bound.
A program may use at most 64 MiB of HBM per device.

v0:
```python
import jax
import jax.numpy as jnp
from jax import lax
from jax.sharding import PartitionSpec as P


def per_device(features, weight, cotangent, counts, columns, live_slots):
    row_count = features.shape[0]
    feat_width = features.shape[1]
    block_count = columns.shape[0]
    slot_count = columns.shape[1]
    block_size = counts.shape[2]
    section_index = lax.axis_index("section")
    section_count = lax.axis_size("section")
    owner_count = lax.axis_size("row") // section_count
    everything = lax.all_gather(features, "row", axis=0, tiled=True)
    grouped = everything.reshape(owner_count, section_count, row_count, feat_width)
    window = lax.dynamic_index_in_dim(grouped, section_index, 1, keepdims=False)
    window = window.reshape(owner_count * block_count, block_size, feat_width)
    local_cols = columns // block_count // section_count * block_count + columns % block_count
    slot_used = jnp.arange(slot_count, dtype=jnp.int32)[None, :] < live_slots
    masked = jnp.where(slot_used[:, :, None, None], counts, 0)
    degree = jnp.sum(masked, axis=(1, 3)).astype(jnp.float32).reshape(row_count)
    edge_mats = masked.astype(jnp.bfloat16)
    picked = window[local_cols]
    partial_value = jnp.einsum(
        "rkij,rkjf->rif", edge_mats, picked, preferred_element_type=jnp.float32
    )
    partial_value = partial_value.reshape(row_count, feat_width)
    summed, degree_all = lax.psum((partial_value, degree), "section")
    aggregate = (summed * lax.rsqrt(1.0 + degree_all)[:, None]).astype(jnp.bfloat16)
    pre_act = jnp.dot(aggregate, weight, preferred_element_type=jnp.float32)
    gate_value = jax.nn.sigmoid(pre_act)
    output = (pre_act * gate_value).astype(jnp.bfloat16)
    grad_pre = (
        cotangent.astype(jnp.float32) * gate_value * (1.0 + pre_act * (1.0 - gate_value))
    ).astype(jnp.bfloat16)
    grad_local = lax.dot_general(
        aggregate, grad_pre, (((0,), (0,)), ((), ())), preferred_element_type=jnp.float32
    )
    grad_weight = lax.psum(grad_local, "row")
    return (output, grad_weight)


def solution(mesh):
    in_specs = (
        P("row", None),
        P(),
        P("row", None),
        P("row", "section", None, None),
        P("row", "section"),
        P("row", "section"),
    )
    out_specs = (P("row", None), P())
    return jax.shard_map(
        per_device, mesh=mesh, in_specs=in_specs, out_specs=out_specs, check_vma=False
    )
```

profile of v0, /device:TPU:0, one launch (start us, length us, event | category | flops | bytes accessed | tf_op | source)
XLA Modules:
  0.0 172.0 jit_solution(4953633193396426414)
XLA Ops:
  7.2 0.0 copy-start
  7.2 0.0 all-gather.2.cloned.1.call-start
  7.2 0.7 all-gather.2.cloned.1.call-update
  7.9 0.0 all-reduce.3.cloned.1.call-start
  8.0 0.7 compare_select_fusion
  8.7 0.1 copy.9
  8.8 0.1 reshape.45
  8.8 0.7 iota_compare_fusion
  9.6 39.8 %all-gather.2.cloned.1.call-done = bf16[8192,256]{1,0:T(8,128)(2,1)} async-done(((bf16[1024,256]{1,0:T(8,128)(2,1)}), bf16[8192,256]{1,0:T(8,128)(2,1)}) %all-gather.2.cloned.1.call-update) | async-done | bytes 4194320 | tf_op jit(solution)/shard_map/all_gather | solution.py:16
  49.4 1.3 constant_dynamic-slice_fusion
  50.6 0.7 gather_fusion
  51.3 3.2 %fusion = f32[8,128,256,1]{2,1,3,0:T(8,128)} fusion(bf16[8,4,128,256]{3,2,1,0:T(8,128)(2,1)S(1)} %bitcast.13, s32[8,4,128,128]{3,2,1,0:T(8,128)} %param.9, pred[8,4]{1,0:T(8,128)(4,1)S(1)} %iota_compare_fusion), kind=kOutput, calls=%fused_computation.3 | convolution fusion | flops 269484032 | bytes 5242912 | tf_op jit(solution)/shard_map/rkij,rkjf->rif/dot_general | solution.py:26
  54.5 0.0 all-reduce.3.cloned.1.call-update
  54.5 0.0 all-reduce.5.cloned.1.call-start
  54.6 1.9 %select_reduce_fusion = s32[8,128]{1,0:T(8,128)S(1)} fusion(s32[8,4,128,128]{3,2,1,0:T(8,128)} %param.9, pred[8,4]{1,0:T(8,128)(4,1)S(1)} %iota_compare_fusion), kind=kLoop, calls=%fused_computation.1 | loop fusion | flops 1047552 | bytes 2101280 | tf_op jit(solution)/shard_map/reduce_sum | solution.py:23
  56.5 11.9 %psum.22 = f32[1024]{0:T(1024)S(1)} all-reduce(f32[1024]{0:T(1024)S(1)} %convert_bitcast_fusion), channel_id=1, replica_groups=mesh['row'=8,'section'=4] {'section'}, use_global_device_ids=true, to_apply=%region_2.3 | all-reduce | flops 1024 | bytes 8192 | tf_op jit(solution)/shard_map/psum | solution.py:30
  68.5 0.0 copy-start.2
  68.5 38.2 %all-reduce.3.cloned.1.call-done = f32[1024,256]{1,0:T(8,128)} async-done(((f32[1024,256]{1,0:T(8,128)}), f32[1024,256]{1,0:T(8,128)}) %all-reduce.3.cloned.1.call-update) | async-done | bytes 1048592 | tf_op jit(solution)/shard_map/psum | solution.py:30
  106.6 0.0 copy-done
  106.6 0.0 copy-start.1
  106.6 2.6 %multiply_convert_fusion.1 = (bf16[1024,256]{1,0:T(8,128)(2,1)}, f32[1024,256]{1,0:T(8,128)S(1)}) fusion(bf16[256,256]{1,0:T(8,128)(2,1)S(1)} %copy-done, f32[1024,256]{1,0:T(8,128)} %all-reduce.3.cloned.1.call-done, f32[1024]{0:T(1024)S(1)} %add_rsqrt_fusion), kind=kOutput, calls=%fused_computation.5 | convolution fusion | flops 136052736 | bytes 2756608 | tf_op jit(solution)/shard_map/dot_general | solution.py:32
  109.2 0.0 copy-done.2
  109.2 0.0 copy-done.1
  109.2 1.5 fusion.3
  110.7 0.0 all-reduce.5.cloned.1.call-update
  110.7 53.1 %all-reduce.5.cloned.1.call-done = f32[256,256]{1,0:T(8,128)} async-done(((f32[256,256]{1,0:T(8,128)}), f32[256,256]{1,0:T(8,128)}) %all-reduce.5.cloned.1.call-update) | async-done | bytes 262160 | tf_op jit(solution)/shard_map/psum | solution.py:41
  163.8 1.7 copy.13
  (3 shorter events, 0.0 us)
Async XLA Ops:
  7.2 99.5 %copy-start = (bf16[256,256]{1,0:T(8,128)(2,1)S(1)}, bf16[256,256]{1,0:T(8,128)(2,1)}, u32[]{:S(2)}) copy-start(bf16[256,256]{1,0:T(8,128)(2,1)} %param.7) | copy-start | bytes 393220
  7.2 42.2 %all-gather.2.cloned.1.call-start = ((), (), s32[]{:S(2)}) async-start(), calls=%async_computation | async-start | bytes 4718592 | tf_op jit(solution)/shard_map/all_gather | solution.py:16
  7.9 98.7 %all-reduce.3.cloned.1.call-start = ((), (), s32[]{:S(2)}) async-start(), calls=%async_computation.1 | async-start | bytes 2097152 | tf_op jit(solution)/shard_map/psum | solution.py:30
  54.5 109.3 %all-reduce.5.cloned.1.call-start = ((), (), s32[]{:S(2)}) async-start(), calls=%async_computation.2 | async-start | bytes 524288 | tf_op jit(solution)/shard_map/psum | solution.py:41
  68.5 40.8 %copy-start.2 = (bf16[1024,256]{1,0:T(8,128)(2,1)S(1)}, bf16[1024,256]{1,0:T(8,128)(2,1)}, u32[]{:S(2)}) copy-start(bf16[1024,256]{1,0:T(8,128)(2,1)} %param.8) | copy-start | bytes 1572868
  106.6 2.6 %copy-start.1 = (f32[1024,256]{1,0:T(8,128)S(1)}, f32[1024,256]{1,0:T(8,128)}, u32[]{:S(2)}) copy-start(f32[1024,256]{1,0:T(8,128)} %all-reduce.3.cloned.1.call-done) | copy-start | bytes 3145732
Sparse Core Ops, SparseCore 0:
  9.9 39.4 all-gather.1
  54.7 51.9 all-reduce.2
  110.8 52.9 all-reduce.4
where the time goes:
time: 172 us
  waiting for transfers between devices  132 us (77%)
  between operations  13.8 us (8%)
  blocking collectives  11.9 us (7%)
  matrix products  7.25 us (4%)
  local copies, waits for them, and re-layouts  3.82 us (2%)
  other arithmetic  3.35 us (2%)
    psum x1, waiting for transfers between devices, per_device(): grad_weight = lax.psum(grad_local, 'row')  53.1 us
    all_gather x1, waiting for transfers between devices, per_device(): everything = lax.all_gather(features, 'row', axis=0, tiled=True)  39.8 us
    psum x1, waiting for transfers between devices, per_device(): summed, degree_all = lax.psum((partial_value, degree), 'section')  38.2 us
    psum x1, blocking collectives, per_device(): summed, degree_all = lax.psum((partial_value, degree), 'section')  11.9 us
  transfers between devices with their start and end apart: 3, of which 3 were waited for; matrix products, arithmetic and copies ran while one was open for 2% of the time, Pallas kernels for 0%

commit v1 on v0

--- a/solution.py
+++ b/solution.py
@@ -38,7 +38,7 @@
     grad_local = lax.dot_general(
         aggregate, grad_pre, (((0,), (0,)), ((), ())), preferred_element_type=jnp.float32
     )
-    grad_weight = lax.psum(grad_local, "row")
+    grad_weight = jnp.sum(lax.all_gather(grad_local, "row"), axis=0)
     return (output, grad_weight)
 
 

time: 172 us -> 147 us (0.85)
  waiting for transfers between devices: 132 us -> 106 us
  other arithmetic: 3.35 us -> 5.8 us
    psum x1 -> x0, waiting for transfers between devices: 53.1 us -> none  [per_device(): grad_weight = lax.psum(grad_local, 'row')]
    all_gather x0 -> x1, waiting for transfers between devices: none -> 27.4 us  [per_device(): grad_weight = jnp.sum(lax.all_gather(grad_local, 'row'), axis=0)]
    reduce_sum x0 -> x1, other arithmetic: none -> 2.45 us  [per_device(): grad_weight = jnp.sum(lax.all_gather(grad_local, 'row'), axis=0)]
where the time goes in v1:
time: 147 us
  waiting for transfers between devices  106 us (72%)
  between operations  13.8 us (9%)
  blocking collectives  11.9 us (8%)
  matrix products  7.25 us (5%)
  other arithmetic  5.8 us (4%)
  local copies, waits for them, and re-layouts  2.16 us (1%)
    all_gather x1, waiting for transfers between devices, per_device(): everything = lax.all_gather(features, 'row', axis=0, tiled=True)  39.8 us
    psum x1, waiting for transfers between devices, per_device(): summed, degree_all = lax.psum((partial_value, degree), 'section')  38.2 us
    all_gather x1, waiting for transfers between devices, per_device(): grad_weight = jnp.sum(lax.all_gather(grad_local, 'row'), axis=0)  27.4 us
    psum x1, blocking collectives, per_device(): summed, degree_all = lax.psum((partial_value, degree), 'section')  11.9 us
    dot_general x1, matrix products, per_device(): jnp.einsum('rkij,rkjf->rif', edge_mats, picked, preferred_element_type=jn...  3.18 us
  transfers between devices with their start and end apart: 3, of which 3 were waited for; matrix products, arithmetic and copies ran while one was open for 2% of the time, Pallas kernels for 0%

profile of v1, /device:TPU:0, one launch (start us, length us, event | category | flops | bytes accessed | tf_op | source)
XLA Modules:
  0.0 147.1 jit_solution(10636196471126940694)
XLA Ops:
  7.2 0.0 copy-start
  7.2 0.0 all-gather.4.cloned.1.call-start
  7.2 0.7 all-gather.4.cloned.1.call-update
  7.9 0.0 all-reduce.2.cloned.1.call-start
  8.0 0.7 compare_select_fusion
  8.7 0.1 copy.9
  8.8 0.1 reshape.45
  8.8 0.7 iota_compare_fusion
  9.6 39.8 %all-gather.4.cloned.1.call-done = bf16[8192,256]{1,0:T(8,128)(2,1)} async-done(((bf16[1024,256]{1,0:T(8,128)(2,1)}), bf16[8192,256]{1,0:T(8,128)(2,1)}) %all-gather.4.cloned.1.call-update) | async-done | bytes 4194320 | tf_op jit(solution)/shard_map/all_gather | solution.py:16
  49.4 1.3 constant_dynamic-slice_fusion
  50.6 0.7 gather_fusion
  51.3 3.2 %fusion = f32[8,128,256,1]{2,1,3,0:T(8,128)} fusion(bf16[8,4,128,256]{3,2,1,0:T(8,128)(2,1)S(1)} %bitcast.14, s32[8,4,128,128]{3,2,1,0:T(8,128)} %param.9, pred[8,4]{1,0:T(8,128)(4,1)S(1)} %iota_compare_fusion), kind=kOutput, calls=%fused_computation.3 | convolution fusion | flops 269484032 | bytes 5242912 | tf_op jit(solution)/shard_map/rkij,rkjf->rif/dot_general | solution.py:26
  54.5 0.0 all-reduce.2.cloned.1.call-update
  54.5 0.0 all-gather.6.cloned.1.call-start
  54.6 1.9 %select_reduce_fusion = s32[8,128]{1,0:T(8,128)S(1)} fusion(s32[8,4,128,128]{3,2,1,0:T(8,128)} %param.9, pred[8,4]{1,0:T(8,128)(4,1)S(1)} %iota_compare_fusion), kind=kLoop, calls=%fused_computation.1 | loop fusion | flops 1047552 | bytes 2101280 | tf_op jit(solution)/shard_map/reduce_sum | solution.py:23
  56.5 11.9 %psum.15 = f32[1024]{0:T(1024)S(1)} all-reduce(f32[1024]{0:T(1024)S(1)} %convert_bitcast_fusion), channel_id=1, replica_groups=mesh['row'=8,'section'=4] {'section'}, use_global_device_ids=true, to_apply=%region_2.3 | all-reduce | flops 1024 | bytes 8192 | tf_op jit(solution)/shard_map/psum | solution.py:30
  68.5 0.0 copy-start.2
  68.5 38.2 %all-reduce.2.cloned.1.call-done = f32[1024,256]{1,0:T(8,128)} async-done(((f32[1024,256]{1,0:T(8,128)}), f32[1024,256]{1,0:T(8,128)}) %all-reduce.2.cloned.1.call-update) | async-done | bytes 1048592 | tf_op jit(solution)/shard_map/psum | solution.py:30
  106.6 0.0 copy-done
  106.6 0.0 copy-start.1
  106.6 2.6 %multiply_convert_fusion.1 = (bf16[1024,256]{1,0:T(8,128)(2,1)}, f32[1024,256]{1,0:T(8,128)S(1)}) fusion(bf16[256,256]{1,0:T(8,128)(2,1)S(1)} %copy-done, f32[1024,256]{1,0:T(8,128)} %all-reduce.2.cloned.1.call-done, f32[1024]{0:T(1024)S(1)} %add_rsqrt_fusion), kind=kOutput, calls=%fused_computation.5 | convolution fusion | flops 136052736 | bytes 2756608 | tf_op jit(solution)/shard_map/dot_general | solution.py:32
  109.2 0.0 copy-done.2
  109.2 0.0 copy-done.1
  109.2 1.5 fusion.3
  110.7 0.0 all-gather.6.cloned.1.call-update
  110.7 27.4 %all-gather.6.cloned.1.call-done = f32[2048,256]{1,0:T(8,128)} async-done(((f32[256,256]{1,0:T(8,128)}), f32[2048,256]{1,0:T(8,128)}) %all-gather.6.cloned.1.call-update) | async-done | bytes 2097168 | tf_op jit(solution)/shard_map/all_gather | solution.py:41
  138.2 2.5 %reduce_sum.19 = f32[256,256]{1,0:T(8,128)} reduce(f32[8,256,256]{2,1,0:T(8,128)} %bitcast.16, f32[]{:T(128)} %constant.56.clone.1), dimensions={0}, to_apply=%region_3.4 | reduce | flops 458752 | bytes 2359300 | tf_op jit(solution)/shard_map/reduce_sum | solution.py:41
  (3 shorter events, 0.0 us)
Async XLA Ops:
  7.2 99.5 %copy-start = (bf16[256,256]{1,0:T(8,128)(2,1)S(1)}, bf16[256,256]{1,0:T(8,128)(2,1)}, u32[]{:S(2)}) copy-start(bf16[256,256]{1,0:T(8,128)(2,1)} %param.7) | copy-start | bytes 393220
  7.2 42.2 %all-gather.4.cloned.1.call-start = ((), (), s32[]{:S(2)}) async-start(), calls=%async_computation | async-start | bytes 4718592 | tf_op jit(solution)/shard_map/all_gather | solution.py:16
  7.9 98.7 %all-reduce.2.cloned.1.call-start = ((), (), s32[]{:S(2)}) async-start(), calls=%async_computation.1 | async-start | bytes 2097152 | tf_op jit(solution)/shard_map/psum | solution.py:30
  54.5 83.6 %all-gather.6.cloned.1.call-start = ((), (), s32[]{:S(2)}) async-start(), calls=%async_computation.2 | async-start | bytes 2359296 | tf_op jit(solution)/shard_map/all_gather | solution.py:41
  68.5 40.8 %copy-start.2 = (bf16[1024,256]{1,0:T(8,128)(2,1)S(1)}, bf16[1024,256]{1,0:T(8,128)(2,1)}, u32[]{:S(2)}) copy-start(bf16[1024,256]{1,0:T(8,128)(2,1)} %param.8) | copy-start | bytes 1572868
  106.6 2.6 %copy-start.1 = (f32[1024,256]{1,0:T(8,128)S(1)}, f32[1024,256]{1,0:T(8,128)}, u32[]{:S(2)}) copy-start(f32[1024,256]{1,0:T(8,128)} %all-reduce.2.cloned.1.call-done) | copy-start | bytes 3145732
Sparse Core Ops, SparseCore 0:
  9.9 39.4 all-gather.3
  54.7 51.9 all-reduce.1
  110.8 27.2 all-gather.5
